TPU v7x, 256 devices: a whole 4x4x8 slice. The times are simulated.
256 devices in a mesh: owner: 8 (over y, core), group: 32 (over z, x).
Axes of the slice: x: 4, y: 4, z: 8, core: 2. Of those that a mesh axis runs over, the one named last changes fastest.
Arguments:
- amplitudes: bfloat16 [1024, 32768], P('group', 'owner'), may hold values from -6 to 6
- integrals: bfloat16 [32768, 32768], P('owner', 'group'), may hold values from -0.09375 to 0.09375
- occ_irrep: int32 [100], replicated, may hold values from 0 to 7
- vir_irrep: int32 [1200], replicated, may hold values from 0 to 7, as said below
- cd_list: int32 [2, 32768], P(None, 'owner'), may hold values from 0 to 1199
- ab_list: int32 [2, 32768], P(None, 'group'), may hold values from 0 to 1199, as said below
Outputs:
- ladder: bfloat16 [1024, 32768], P('owner', 'group')
Inputs may be any that keep to these rules, and one draw needn't show every extreme that they name: `vir_irrep`: irrep labels of D2h; each of the 8 labels occurs. `occ_irrep`: irrep labels of D2h. `cd_list`: indices of virtual orbitals. `ab_list`: indices of virtual orbitals; the residual pairs of each index of group form 8 consecutive blocks of 128 pairs, and every pair (a,b) of block k has vir_irrep[a] XOR vir_irrep[b] == k.
All inputs are finite; a program needn't handle non-finite values.
Results may differ from a plain program's by a relative error of at most 0.001.
Values may be sent and summed in bfloat16 or wider, within the bound.
No kernel may reach another device: no remote copies, remote signals or barrier semaphores. Data moves between devices by JAX's collectives and lax.ppermute only.
A program may use at most 64 MiB of HBM per device.

v0:
```python
import jax
import jax.numpy as jnp
from jax import lax
from jax.sharding import PartitionSpec as P


def label_lookup(indices, table):
    count = table.shape[0]
    columns = jnp.arange(count, dtype=jnp.int32)
    onehot = (indices[:, None] == columns[None, :]).astype(jnp.bfloat16)
    values = jnp.dot(
        onehot, table.astype(jnp.bfloat16)[:, None], preferred_element_type=jnp.float32
    )
    return values[:, 0].astype(jnp.int32)


def pair_irreps(pair_list, table):
    length = pair_list.shape[1]
    both = label_lookup(pair_list.reshape(2 * length), table)
    return jnp.bitwise_xor(both[:length], both[length:])


def local(amplitudes, integrals, occ_irrep, vir_irrep, cd_list, ab_list):
    sym_cd = pair_irreps(cd_list, vir_irrep)
    sym_ab = pair_irreps(ab_list, vir_irrep)
    total_pairs = amplitudes.shape[0] * lax.axis_size("group")
    occupied = occ_irrep.shape[0]
    rows = jnp.arange(total_pairs, dtype=jnp.int32)
    row_pairs = jnp.concatenate([rows // occupied, rows % occupied])
    both_occ = label_lookup(row_pairs, occ_irrep)
    sym_ij = jnp.bitwise_xor(both_occ[:total_pairs], both_occ[total_pairs:])
    weights = jnp.where(
        sym_cd[:, None] == sym_ab[None, :], integrals, jnp.zeros((), integrals.dtype)
    )
    gathered = lax.all_gather(amplitudes, "group", axis=0, tiled=True)
    selected = jnp.where(
        sym_ij[:, None] == sym_cd[None, :], gathered, jnp.zeros((), gathered.dtype)
    )
    product = jnp.dot(selected, weights, preferred_element_type=jnp.float32)
    reduced = lax.psum_scatter(product, "owner", scatter_dimension=0, tiled=True)
    return reduced.astype(jnp.bfloat16)


def solution(mesh):
    return jax.shard_map(
        local,
        mesh=mesh,
        in_specs=(
            P("group", "owner"),
            P("owner", "group"),
            P(),
            P(),
            P(None, "owner"),
            P(None, "group"),
        ),
        out_specs=P("owner", "group"),
        check_vma=False,
    )
```

profile of v0, /device:TPU:2, one launch (start us, length us, event | category | flops | bytes accessed | tf_op | source)
XLA Modules:
  0.0 173.8 jit_solution(6140189908563980151)
XLA Ops:
  6.5 0.0 all-gather.2.cloned.1.call-start
  6.5 0.7 all-gather.2.cloned.1.call-update
  7.3 0.0 reduce-scatter.2.cloned.1.call-start
  7.3 0.7 convert_element_type.24
  8.0 0.7 copy.10
  8.7 2.2 %fusion.2 = f32[1,2048]{1,0:T(1,128)S(1)} fusion(bf16[1200,1]{0,1:T(2,128)(2,1)S(1)} %reshape.21, s32[2048]{0:T(1024)S(1)} %bitcast.20), kind=kOutput, calls=%fused_computation.6 | convolution fusion | flops 7372800 | bytes 18784 | tf_op jit(solution)/shard_map/dot_general | solution.py:11
  10.9 1.1 fusion.11
  12.1 0.8 copy.7
  12.8 5.8 %fusion = f32[1,8192]{1,0:T(1,128)S(1)} fusion(bf16[1200,1]{0,1:T(2,128)(2,1)S(1)} %reshape.21, s32[8192]{0:T(1024)S(1)} %bitcast.16), kind=kOutput, calls=%fused_computation.1 | convolution fusion | flops 29491200 | bytes 67936 | tf_op jit(solution)/shard_map/dot_general | solution.py:11
  18.7 90.8 %all-gather.2.cloned.1.call-done = bf16[1024,4096]{1,0:T(8,128)(2,1)} async-done(((bf16[32,4096]{1,0:T(8,128)(2,1)}), bf16[1024,4096]{1,0:T(8,128)(2,1)}) %all-gather.2.cloned.1.call-update) | async-done | bytes 8388624 | tf_op jit(solution)/shard_map/all_gather | solution.py:35
  109.5 16.7 %fusion.3 = f32[1024,1024]{1,0:T(8,128)} fusion(bf16[1024,4096]{1,0:T(8,128)(2,1)} %all-gather.2.cloned.1.call-done, bf16[4096,1024]{1,0:T(8,128)(2,1)} %param.7, s32[1024]{0:T(1024)S(1)} %slice_xor_fusion.1, s32[4096]{0:T(1024)S(1)} %slice_xor_fusion, s32[1024]{0:T(1024)S(1)} %slice_xor_fusion.2), kind=kOutput, calls=%fused_computation.7 | convolution fusion | flops 8606711808 | bytes 20996096 | tf_op jit(solution)/shard_map/dot_general | solution.py:39
  126.1 0.0 reduce-scatter.2.cloned.1.call-update
  126.2 39.1 %reduce-scatter.2.cloned.1.call-done = f32[128,1024]{1,0:T(8,128)} async-done(((f32[1024,1024]{1,0:T(8,128)}), f32[128,1024]{1,0:T(8,128)}) %reduce-scatter.2.cloned.1.call-update) | async-done | bytes 524304 | tf_op jit(solution)/shard_map/reduce_scatter | solution.py:40
  165.2 1.8 %convert_element_type.27 = bf16[128,1024]{1,0:T(8,128)(2,1)} convert(f32[128,1024]{1,0:T(8,128)} %reduce-scatter.2.cloned.1.call-done) | non-fusion elementwise | flops 131072 | bytes 786432 | tf_op jit(solution)/shard_map/convert_element_type | solution.py:41
  (9 shorter events, 0.1 us)
Async XLA Ops:
  6.5 103.0 %all-gather.2.cloned.1.call-start = ((), (), s32[]{:S(2)}) async-start(), calls=%async_computation.1 | async-start | bytes 8650752 | tf_op jit(solution)/shard_map/all_gather | solution.py:35
  7.3 158.0 %reduce-scatter.2.cloned.1.call-start = ((), (), s32[]{:S(2)}) async-start(), calls=%async_computation.2 | async-start | bytes 4718592 | tf_op jit(solution)/shard_map/reduce_scatter | solution.py:40
Sparse Core Ops, SparseCore 0:
  9.9 99.5 all-gather.1
  126.3 38.8 reduce-scatter.1
where the time goes:
time: 174 us
  waiting for transfers between devices  131 us (75%)
  matrix products  25.8 us (15%)
  between operations  13.4 us (8%)
  other arithmetic  2.53 us (1%)
    all_gather x1, waiting for transfers between devices, local(): gathered = lax.all_gather(amplitudes, 'group', axis=0, tiled=True)  90.8 us
    reduce_scatter x1, waiting for transfers between devices, local(): lax.psum_scatter(product, 'owner', scatter_dimension=0, tiled=True)  39.1 us
    dot_general x1, matrix products, local(): product = jnp.dot(selected, weights, preferred_element_type=jnp.float32)  16.7 us
    dot_general x3, matrix products, label_lookup(): jnp.dot(onehot, table.astype(jnp.bfloat16)[:, None], preferred_element_ty...  9.14 us
  transfers between devices with their start and end apart: 2, of which 2 were waited for; matrix products, arithmetic and copies ran while one was open for 7% of the time, Pallas kernels for 0%

commit v1 on v0

--- a/solution.py
+++ b/solution.py
@@ -32,7 +32,9 @@
     weights = jnp.where(
         sym_cd[:, None] == sym_ab[None, :], integrals, jnp.zeros((), integrals.dtype)
     )
-    gathered = lax.all_gather(amplitudes, "group", axis=0, tiled=True)
+    gathered = jnp.concatenate(
+        lax.all_to_all(jnp.stack([amplitudes] * lax.axis_size("group")), "group", 0, 0), axis=0
+    )
     selected = jnp.where(
         sym_ij[:, None] == sym_cd[None, :], gathered, jnp.zeros((), gathered.dtype)
     )

time: 174 us -> 284 us (1.63)
  waiting for transfers between devices: 131 us -> 226 us
  starting transfers between devices: 0.04 us -> 11.8 us
  local copies, waits for them, and re-layouts: 1.47 us -> 5.25 us
    all_to_all x0 -> x1, waiting for transfers between devices: none -> 182 us  [local(): lax.all_to_all(jnp.stack([amplitudes] * lax.axis_size('group')), 'group',...]
    all_gather x1 -> x0, waiting for transfers between devices: 90.8 us -> none  [local(): gathered = lax.all_gather(amplitudes, 'group', axis=0, tiled=True)]
    all_to_all x0 -> x1, starting transfers between devices: none -> 11.8 us  [local(): lax.all_to_all(jnp.stack([amplitudes] * lax.axis_size('group')), 'group',...]
    reduce_scatter x1, waiting for transfers between devices: 39.1 us -> 44.9 us  [local(): lax.psum_scatter(product, 'owner', scatter_dimension=0, tiled=True)]
    another operation x0 -> x1, local copies, waits for them, and re-layouts: none -> 5.22 us  [local(): jnp.stack([amplitudes] * lax.axis_size('group'))]
  transfers between devices with their start and end apart: 2 -> 2, of which waited for: 2 -> 2; matrix products, arithmetic and copies ran while one was open for 7% -> 3% of each run, Pallas kernels for 0% -> 0%
where the time goes in v1:
time: 284 us
  waiting for transfers between devices  226 us (80%)
  matrix products  25.3 us (9%)
  between operations  13.5 us (5%)
  starting transfers between devices  11.8 us (4%)
  local copies, waits for them, and re-layouts  5.25 us (2%)
    all_to_all x1, waiting for transfers between devices, local(): lax.all_to_all(jnp.stack([amplitudes] * lax.axis_size('group')), 'group',...  182 us
    reduce_scatter x1, waiting for transfers between devices, local(): lax.psum_scatter(product, 'owner', scatter_dimension=0, tiled=True)  44.9 us
    dot_general x1, matrix products, local(): product = jnp.dot(selected, weights, preferred_element_type=jnp.float32)  16.7 us
    all_to_all x1, starting transfers between devices, local(): lax.all_to_all(jnp.stack([amplitudes] * lax.axis_size('group')), 'group',...  11.8 us
    dot_general x3, matrix products, label_lookup(): jnp.dot(onehot, table.astype(jnp.bfloat16)[:, None], preferred_element_ty...  8.59 us
  transfers between devices with their start and end apart: 2, of which 2 were waited for; matrix products, arithmetic and copies ran while one was open for 3% of the time, Pallas kernels for 0%

profile of v1, /device:TPU:2, one launch (start us, length us, event | category | flops | bytes accessed | tf_op | source)
XLA Modules:
  0.0 284.2 jit_solution(10886669695736260065)
XLA Ops:
  6.5 5.2 %stack.2 = bf16[32,32,4096]{2,1,0:T(8,128)(2,1)} broadcast(bf16[32,4096]{1,0:T(8,128)(2,1)} %param.6), dimensions={1,2} | broadcast | bytes 8650752 | tf_op jit(solution)/shard_map/stack | solution.py:36
  11.8 0.0 copy-start.1
  11.8 0.0 copy-start.2
  11.8 0.0 copy-start
  11.8 11.8 %all-to-all-start = ((bf16[32,32,4096]{2,1,0:T(8,128)(2,1)}), bf16[32,32,4096]{2,1,0:T(8,128)(2,1)}, u32[]{:S(2)}, u32[]{:S(2)}) async-start(bf16[32,32,4096]{2,1,0:T(8,128)(2,1)} %stack.2), calls=%async_computation | async-start | bytes 16777216 | tf_op jit(solution)/shard_map/all_to_all | solution.py:36
  23.6 0.0 copy-start.3
  23.6 0.0 reduce-scatter.2.cloned.1.call-start
  23.6 0.0 copy-done.1
  23.7 0.0 copy-done.2
  23.7 2.3 fusion.2
  26.0 0.0 copy-done
  26.0 5.8 %fusion = f32[1,8192]{1,0:T(1,128)S(1)} fusion(bf16[1200,1]{0,1:T(2,128)(2,1)S(1)} %reshape.27, s32[8192]{0:T(1024)S(1)} %bitcast.17), kind=kOutput, calls=%fused_computation.1 | convolution fusion | flops 29491200 | bytes 67936 | tf_op jit(solution)/shard_map/dot_general | solution.py:11
  31.9 0.0 copy-done.3
  31.9 0.5 fusion.11
  32.4 181.5 %all-to-all-done = bf16[32,32,4096]{2,1,0:T(8,128)(2,1)} async-done(((bf16[32,32,4096]{2,1,0:T(8,128)(2,1)}), bf16[32,32,4096]{2,1,0:T(8,128)(2,1)}, u32[]{:S(2)}, u32[]{:S(2)}) %all-to-all-start) | async-done | bytes 8388640 | tf_op jit(solution)/shard_map/all_to_all | solution.py:36
  213.9 16.7 %fusion.3 = f32[1024,1024]{1,0:T(8,128)} fusion(bf16[1024,4096]{1,0:T(8,128)(2,1)} %bitcast.3, bf16[4096,1024]{1,0:T(8,128)(2,1)} %param.7, s32[1024]{0:T(1024)S(1)} %slice_xor_fusion.1, s32[4096]{0:T(1024)S(1)} %slice_xor_fusion, s32[1024]{0:T(1024)S(1)} %slice_xor_fusion.2), kind=kOutput, calls=%fused_computation.7 | convolution fusion | flops 8606711808 | bytes 20996096 | tf_op jit(solution)/shard_map/dot_general | solution.py:41
  230.6 0.0 reduce-scatter.2.cloned.1.call-update
  230.6 44.9 %reduce-scatter.2.cloned.1.call-done = f32[128,1024]{1,0:T(8,128)} async-done(((f32[1024,1024]{1,0:T(8,128)}), f32[128,1024]{1,0:T(8,128)}) %reduce-scatter.2.cloned.1.call-update) | async-done | bytes 524304 | tf_op jit(solution)/shard_map/reduce_scatter | solution.py:42
  275.5 1.8 convert_element_type.27
  (12 shorter events, 0.1 us)
Async XLA Ops:
  11.8 11.9 %copy-start.1 = (s32[1200]{0:T(1024)S(1)}, s32[1200]{0:T(1024)}, u32[]{:S(2)}) copy-start(s32[1200]{0:T(1024)} %param.9) | copy-start | bytes 14404
  11.8 11.9 %copy-start.2 = (s32[2,1024]{1,0:T(2,128)S(1)}, s32[2,1024]{1,0:T(2,128)}, u32[]{:S(2)}) copy-start(s32[2,1024]{1,0:T(2,128)} %param.11) | copy-start | bytes 24580
  11.8 14.3 %copy-start = (s32[2,4096]{1,0:T(2,128)S(1)}, s32[2,4096]{1,0:T(2,128)}, u32[]{:S(2)}) copy-start(s32[2,4096]{1,0:T(2,128)} %param.10) | copy-start | bytes 98308
  11.8 202.1 %all-to-all-start = ((bf16[32,32,4096]{2,1,0:T(8,128)(2,1)}), bf16[32,32,4096]{2,1,0:T(8,128)(2,1)}, u32[]{:S(2)}, u32[]{:S(2)}) async-start(bf16[32,32,4096]{2,1,0:T(8,128)(2,1)} %stack.2), calls=%async_computation | async-start | bytes 16777216 | tf_op jit(solution)/shard_map/all_to_all | solution.py:36
  23.6 8.3 %copy-start.3 = (s32[100]{0:T(128)S(1)}, s32[100]{0:T(128)}, u32[]{:S(2)}) copy-start(s32[100]{0:T(128)} %param.8) | copy-start | bytes 1204
  23.6 252.0 %reduce-scatter.2.cloned.1.call-start = ((), (), s32[]{:S(2)}) async-start(), calls=%async_computation.2 | async-start | bytes 4718592 | tf_op jit(solution)/shard_map/reduce_scatter | solution.py:42
Sparse Core Ops, SparseCore 0:
  230.7 44.7 reduce-scatter.1
